TPU v7x, 128 devices: a whole 4x4x4 slice. The times are simulated.
128 devices in a mesh: pool: 8 (over x, core), wide: 8 (over y, z_hi), narrow: 2 (over z_lo).
Axes of the slice: x: 4, y: 4, z: 4 (z_hi: 2, z_lo: 2; z = z_hi * 2 + z_lo), core: 2. Of those that a mesh axis runs over, the one named last changes fastest.
Arguments:
- states: bfloat16 [384, 2560], P('pool'), may hold values from -3 to 3
- gain_in: float32 [2560], replicated, may hold values from 0.1 to 1.9
- w_qkv: bfloat16 [2560, 8, 6, 128], P('narrow', 'wide'), may hold values from -0.125 to 0.125
- q_gain: float32 [128], replicated, may hold values from 0.1 to 1.9
- k_gain: float32 [128], replicated, may hold values from 0.1 to 1.9
- key_cache: bfloat16 [2304, 8, 128, 128], P('pool', 'wide', 'narrow'), as said below
- value_cache: bfloat16 [2304, 8, 128, 128], P('pool', 'wide', 'narrow'), may hold values from -12 to 12
- cache_len: int32 [384], replicated, may hold values from 1 to 8192, as said below
- page_table: int32 [384, 64], replicated, may hold values from -1 to 2303, as said below
- w_out: bfloat16 [4096, 2560], P('wide'), may hold values from -0.125 to 0.125
- gain_post: float32 [2560], replicated, may hold values from 0.1 to 1.9
- w_gate_up: bfloat16 [2560, 2, 9728], P(None, None, ('wide', 'narrow')), may hold values from -0.125 to 0.125
- w_down: bfloat16 [9728, 2560], P(('wide', 'narrow')), may hold values from -0.078125 to 0.078125
Outputs:
- attn_mixed: bfloat16 [384, 2560], P('pool')
- layer_out: bfloat16 [384, 2560], P('pool')
Inputs may be any that keep to these rules, and one draw needn't show every extreme that they name: `cache_len`: exactly one request has 8192 cached tokens; every other request has at most (5) * 128. `page_table`: entry (r, b) is pool device times 288 plus slot of the page with tokens b * 128 to (b + 1) * 128 - 1 of request r for b < ceil(cache_len[r] / 128), and -1 for later b; no slot is named twice. One pool device holds exactly 288 pages; the others hold the remaining pages, within one page of each other. `key_cache`: cached keys.
All inputs are finite; a program needn't handle non-finite values.
Results may differ from a plain program's by a relative error of at most 0.012.
The roundings to bfloat16 on the way count: a program that leaves them out, or rounds other values in their place, can miss the bound.
Values may be sent and summed in bfloat16 or wider, within the bound.
No kernel may reach another device: no remote copies, remote signals or barrier semaphores. Data moves between devices by JAX's collectives and lax.ppermute only.
A program may use at most 128 MiB of HBM per device.

v0:
```python
import math
import jax
import jax.numpy as jnp
from jax import lax
from jax.sharding import PartitionSpec as P

epsilon = 1e-06
rope_base = 1000000.0
masked_score = -1e30


def rms_scale(values, gain):
    return values * lax.rsqrt(jnp.mean(values * values, axis=-1, keepdims=True) + epsilon) * gain


def rotate(values, angle_pos):
    half = values.shape[-1] // 2
    ramp = jnp.arange(half).astype(jnp.float32)
    freqs = jnp.exp(ramp * (-2.0 * math.log(rope_base) / values.shape[-1]))
    angle = angle_pos[..., None] * freqs
    cosine = jnp.cos(angle)
    sine = jnp.sin(angle)
    lower = values[..., :half]
    upper = values[..., half:]
    return jnp.concatenate([lower * cosine - upper * sine, upper * cosine + lower * sine], axis=-1)


def feed_forward(normed_post, w_gate_up):
    gate_up = jnp.einsum("rd,dcf->rcf", normed_post, w_gate_up, preferred_element_type=jnp.float32)
    return (jax.nn.silu(gate_up[:, 0]) * gate_up[:, 1]).astype(jnp.bfloat16)


def per_device(
    states,
    gain_in,
    w_qkv,
    q_gain,
    k_gain,
    key_cache,
    value_cache,
    cache_len,
    page_table,
    w_out,
    gain_post,
    w_gate_up,
    w_down,
):
    kv_local = w_qkv.shape[1]
    group = w_qkv.shape[2] - 2
    head_dim = w_qkv.shape[3]
    scale = head_dim ** (-0.5)
    narrow_size = lax.axis_size("narrow")
    narrow_index = lax.axis_index("narrow")
    pool_index = lax.axis_index("pool")
    resid_in = states.astype(jnp.float32)
    normed = rms_scale(resid_in, gain_in).astype(jnp.bfloat16)
    part_width = w_qkv.shape[0]
    own_part = lax.dynamic_slice_in_dim(normed, narrow_index * part_width, part_width, 1)
    partial_proj = jnp.einsum("rd,dkch->rkch", own_part, w_qkv, preferred_element_type=jnp.float32)
    proj = lax.psum_scatter(partial_proj, "narrow", scatter_dimension=0, tiled=True)
    row_count = proj.shape[0]
    first_row = (pool_index * narrow_size + narrow_index) * row_count
    own_len = lax.dynamic_slice_in_dim(cache_len, first_row, row_count, 0)
    position = own_len.astype(jnp.float32)
    query = rotate(
        rms_scale(proj[:, :, :group], q_gain),
        jnp.broadcast_to(position[:, None, None], (row_count, kv_local, group)),
    ).astype(jnp.bfloat16)
    key_new = rotate(rms_scale(proj[:, :, group], k_gain), position[:, None]).astype(jnp.bfloat16)
    value_new = proj[:, :, group + 1].astype(jnp.bfloat16)
    all_queries = lax.all_gather(query, ("pool", "narrow"), axis=0, tiled=True)
    slot_count = key_cache.shape[0]
    half_page = key_cache.shape[2]
    holder_count = lax.axis_size("pool")
    req_count = page_table.shape[0]
    max_blocks = page_table.shape[1]
    flat_pages = page_table.reshape(-1)
    entry = jnp.arange(req_count * max_blocks, dtype=jnp.int32)
    target = jnp.where(flat_pages >= 0, flat_pages, holder_count * slot_count)
    owner_all = (
        jnp.full((holder_count * slot_count,), -1, jnp.int32)
        .at[target]
        .set(entry // max_blocks, mode="drop")
    )
    block_all = (
        jnp.zeros((holder_count * slot_count,), jnp.int32)
        .at[target]
        .set(entry % max_blocks, mode="drop")
    )
    owner = lax.dynamic_slice_in_dim(owner_all, pool_index * slot_count, slot_count, 0)
    block = lax.dynamic_slice_in_dim(block_all, pool_index * slot_count, slot_count, 0)
    safe_owner = jnp.maximum(owner, 0)
    page_len = half_page * narrow_size
    token_pos = (
        block[:, None] * page_len
        + narrow_index * half_page
        + jnp.arange(half_page, dtype=jnp.int32)[None, :]
    )
    live = (owner[:, None] >= 0) & (token_pos < cache_len[safe_owner][:, None])
    live_mask = live[:, None, None, :]
    slot_query = all_queries[safe_owner]
    scores = (
        jnp.einsum("skgd,sktd->skgt", slot_query, key_cache, preferred_element_type=jnp.float32)
        * scale
    )
    slot_top = jnp.max(jnp.where(live_mask, scores, masked_score), axis=-1)
    member = owner[:, None] == jnp.arange(req_count, dtype=jnp.int32)[None, :]
    req_top = jnp.max(jnp.where(member[:, :, None, None], slot_top[:, None], masked_score), axis=0)
    expo = jnp.where(live_mask, jnp.exp(scores - req_top[safe_owner][..., None]), 0.0)
    slot_total = jnp.sum(expo, axis=-1)
    slot_out = jnp.einsum(
        "skgt,sktd->skgd",
        expo.astype(jnp.bfloat16),
        value_cache,
        preferred_element_type=jnp.float32,
    )
    member_weight = member.astype(jnp.float32)
    req_out = jnp.einsum(
        "sr,sx->rx",
        member_weight,
        slot_out.reshape(slot_count, -1),
        precision=lax.Precision.HIGHEST,
    )
    req_out = req_out.reshape(req_count, kv_local, group, head_dim)
    req_total = jnp.einsum(
        "sr,sx->rx",
        member_weight,
        slot_total.reshape(slot_count, -1),
        precision=lax.Precision.HIGHEST,
    )
    req_total = req_total.reshape(req_count, kv_local, group)
    got_out, got_top, got_total = (
        lax.all_to_all(req_out[None], ("pool", "narrow"), split_axis=1, concat_axis=0, tiled=True),
        lax.all_to_all(req_top[None], ("pool", "narrow"), split_axis=1, concat_axis=0, tiled=True),
        lax.all_to_all(
            req_total[None], ("pool", "narrow"), split_axis=1, concat_axis=0, tiled=True
        ),
    )
    own_score = (
        jnp.einsum("rkgd,rkd->rkg", query, key_new, preferred_element_type=jnp.float32) * scale
    )
    top = jnp.maximum(jnp.max(got_top, axis=0), own_score)
    factor = jnp.exp(got_top - top[None])
    own_expo = jnp.exp(own_score - top)
    total = jnp.sum(got_total * factor, axis=0) + own_expo
    own_term = jnp.einsum(
        "rkg,rkd->rkgd",
        own_expo.astype(jnp.bfloat16),
        value_new,
        preferred_element_type=jnp.float32,
    )
    summed = jnp.sum(got_out * factor[..., None], axis=0) + own_term
    attn = (
        (summed / total[..., None])
        .astype(jnp.bfloat16)
        .reshape(row_count, kv_local * group * head_dim)
    )
    partial_out = jnp.dot(
        lax.all_gather(attn, "narrow", axis=0, tiled=True),
        w_out,
        preferred_element_type=jnp.float32,
    )
    mixed = lax.psum(partial_out, "wide")
    resid = resid_in + mixed
    attn_mixed = mixed.astype(jnp.bfloat16)
    normed_post = rms_scale(resid, gain_post).astype(jnp.bfloat16)
    hidden = feed_forward(normed_post, w_gate_up)
    down = jnp.dot(hidden, w_down, preferred_element_type=jnp.float32)
    layer_out = (resid + lax.psum(down, ("wide", "narrow"))).astype(jnp.bfloat16)
    return (attn_mixed, layer_out)


def solution(mesh):
    in_specs = (
        P("pool", None),
        P(),
        P("narrow", "wide", None, None),
        P(),
        P(),
        P("pool", "wide", "narrow", None),
        P("pool", "wide", "narrow", None),
        P(),
        P(),
        P("wide", None),
        P(),
        P(None, None, ("wide", "narrow")),
        P(("wide", "narrow"), None),
    )
    out_specs = (P("pool", None), P("pool", None))
    return jax.shard_map(
        per_device, mesh=mesh, in_specs=in_specs, out_specs=out_specs, check_vma=False
    )
```

profile of v0, /device:TPU:0, one launch (start us, length us, event | category | flops | bytes accessed | tf_op | source)
XLA Modules:
  0.0 489.5 jit_solution(1775987561983351854)
XLA Ops:
  7.2 1.2 multiply_reduce_fusion.1
  8.5 1.8 convert_element_type.67
  10.3 0.8 dynamic-slice
  11.0 2.9 fusion.9
  14.0 0.7 fusion.32
  15.1 90.5 %scatter_custom_fusion.1 = s32[2304]{0:T(1024)S(1)} fusion(s32[24576]{0:T(1024)S(1)} %bitcast.105, s32[24576]{0:T(1024)} %fusion.32, s32[]{:T(128)} %constant.29.clone.1), kind=kCustom, calls=%fused_computation.110 | custom fusion | bytes 9728 | tf_op jit(solution)/shard_map/scatter | solution.py:88
  105.6 90.2 %scatter_custom_fusion = s32[2304]{0:T(1024)S(1)} fusion(s32[24576]{0:T(1024)S(1)} %bitcast.106, s32[24576]{0:T(1024)S(1)} %add_select_fusion, s32[]{:T(128)} %constant.28.clone.1), kind=kCustom, calls=%fused_computation.112 | custom fusion | bytes 9220 | tf_op jit(solution)/shard_map/scatter | solution.py:83
  196.0 2.4 gather_fusion
  198.7 0.8 iota_compare_fusion
  199.5 0.8 multiply_reduce_fusion.4
  200.3 0.9 multiply_reduce_fusion.3
  201.2 0.8 multiply_multiply_fusion.1
  202.0 0.7 fusion.76
  202.8 0.9 multiply_multiply_fusion
  203.9 32.0 %all_gather.6 = bf16[384,1,4,128]{3,0,2,1:T(8,128)(2,1)S(1)} all-gather(bf16[24,1,4,128]{3,0,2,1:T(8,128)(2,1)S(1)} %pad_maximum_fusion), channel_id=1, replica_groups=mesh['pool'=8,'wide'=8,'narrow'=2] {'pool','narrow'}, dimensions={0}, use_global_device_ids=true | all-gather | bytes 417792 | tf_op jit(solution)/shard_map/all_gather | solution.py:71
  236.2 2.4 gather_fusion.1
  238.6 5.8 %select_reduce_fusion.1 = (f32[288,4]{1,0:T(8,128)S(1)}, f32[288,4,64]{2,1,0:T(4,128)}) fusion(pred[288,64]{1,0:T(8,128)(4,1)S(1)} %fusion.36, bf16[288,4,128]{2,1,0:T(4,128)(2,1)} %gather_fusion.1, bf16[288,1,64,128]{3,2,1,0:T(8,128)(2,1)} %param.18), kind=kOutput, calls=%fused_computation.23 | convolution fusion | flops 19094400 | bytes 5331456 | tf_op jit(solution)/shard_map/skgd,sktd->skgt/dot_general | solution.py:103
  245.0 0.8 copy.68
  245.8 3.5 all-to-all-start.1
  249.3 1.7 gather_fusion.2
  251.1 1.9 fusion.16
  253.0 4.8 fusion
  257.9 1.4 fusion.29
  259.5 0.8 fusion.58
  260.2 1.3 fusion.70
  261.5 5.6 %all-to-all-start.2 = ((f32[1,384,1,4]{3,2,0,1:T(1,128)}), f32[1,384,1,4]{3,2,0,1:T(1,128)S(1)}, u32[]{:S(2)}, u32[]{:S(2)}) async-start(f32[1,384,1,4]{3,2,0,1:T(1,128)} %bitcast.101), calls=%async_computation.3 | async-start | bytes 393216 | tf_op jit(solution)/shard_map/all_to_all | solution.py:135
  267.2 2.0 convolution_bitcast_fusion
  269.1 1.4 copy.67
  270.5 0.6 reduce_max.32
  271.2 3.5 all-to-all-done.2
  274.7 0.7 copy-done.3
  275.4 4.3 all-to-all-start
  279.7 0.8 multiply_maximum_fusion
  281.1 0.7 subtract_exponential_fusion
  281.8 1.7 copy.69
  283.5 1.0 multiply_reduce_fusion.2
  284.5 0.7 convert_convert_fusion
  285.4 8.9 %all-to-all-done = f32[1,384,1,4,128]{4,3,2,0,1:T(4,128)} async-done(((f32[1,384,1,4,128]{4,3,2,0,1:T(4,128)}), f32[1,384,1,4,128]{4,3,2,0,1:T(4,128)}, u32[]{:S(2)}, u32[]{:S(2)}) %all-to-all-start) | async-done | bytes 786464 | tf_op jit(solution)/shard_map/all_to_all | solution.py:133
  294.3 1.4 fusion.12
  295.7 0.8 copy_bitcast_fusion
  296.5 4.5 all_gather.7
  301.0 3.1 fusion.81
  304.2 85.7 %all-reduce.3.cloned.1.call-done = f32[48,2560]{1,0:T(8,128)} async-done(((f32[48,2560]{1,0:T(8,128)}), f32[48,2560]{1,0:T(8,128)}) %all-reduce.3.cloned.1.call-update) | async-done | bytes 491536 | tf_op jit(solution)/shard_map/psum | solution.py:163
  389.9 1.2 multiply_reduce_fusion
  391.1 4.9 fusion.23
  396.1 1.4 fusion.50
  397.5 83.2 %all-reduce.5.cloned.1.call-done = f32[48,2560]{1,0:T(8,128)} async-done(((f32[48,2560]{1,0:T(8,128)}), f32[48,2560]{1,0:T(8,128)}) %all-reduce.5.cloned.1.call-update) | async-done | bytes 491536 | tf_op jit(solution)/shard_map/psum | solution.py:169
  480.8 2.2 add_convert_fusion
  (70 shorter events, 3.1 us)
Async XLA Ops:
  7.2 388.9 %copy-start = (bf16[608,2560]{1,0:T(8,128)(2,1)S(1)}, bf16[608,2560]{1,0:T(8,128)(2,1)}, u32[]{:S(2)}) copy-start(bf16[608,2560]{1,0:T(8,128)(2,1)} %param.25) | copy-start | bytes 9338884
  7.2 7.4 %copy-start.11 = (s32[384,64]{0,1:T(8,128)S(1)}, s32[384,64]{0,1:T(8,128)}, u32[]{:S(2)}) copy-start(s32[384,64]{0,1:T(8,128)} %param.21) | copy-start | bytes 294916
  7.2 188.8 %copy-start.1 = (s32[384]{0:T(512)S(1)}, s32[384]{0:T(512)}, u32[]{:S(2)}) copy-start(s32[384]{0:T(512)} %param.20) | copy-start | bytes 4612
  7.2 192.3 %reduce-scatter.2.cloned.1.call-start = ((), (), s32[]{:S(2)}) async-start(), calls=%async_computation.4 | async-start | bytes 221184 | tf_op jit(solution)/shard_map/reduce_scatter | solution.py:60
  10.3 192.5 %copy-start.18 = (f32[128]{0:T(128)S(1)}, f32[128]{0:T(128)}, u32[]{:S(2)}) copy-start(f32[128]{0:T(128)} %param.16) | copy-start | bytes 1540
  195.9 40.0 %copy-start.12 = (s32[288]{0:T(512)}, s32[288]{0:T(512)S(1)}, u32[]{:S(2)}) copy-start(s32[288]{0:T(512)S(1)} %get-tuple-element.3) | copy-start | bytes 3460
  195.9 48.5 %copy-start.14 = (s32[1024]{0:T(1024)}, s32[1024]{0:T(1024)S(1)}, u32[]{:S(2)}) copy-start(s32[1024]{0:T(1024)S(1)} %pad_clamp_fusion) | copy-start | bytes 12292
  198.6 45.8 %copy-start.5 = (pred[288,64]{1,0:T(8,128)(4,1)}, pred[288,64]{1,0:T(8,128)(4,1)S(1)}, u32[]{:S(2)}) copy-start(pred[288,64]{1,0:T(8,128)(4,1)S(1)} %fusion.36) | copy-start | bytes 55300
  203.8 32.1 %copy-start.6 = (bf16[24,1,4,64]{3,0,2,1:T(8,128)(2,1)}, bf16[24,1,4,64]{3,0,2,1:T(8,128)(2,1)S(1)}, u32[]{:S(2)}) copy-start(bf16[24,1,4,64]{3,0,2,1:T(8,128)(2,1)S(1)} %get-tuple-element.6) | copy-start | bytes 36868
  203.8 32.1 %copy-start.8 = (bf16[24,1,4,64]{3,0,2,1:T(8,128)(2,1)}, bf16[24,1,4,64]{3,0,2,1:T(8,128)(2,1)S(1)}, u32[]{:S(2)}) copy-start(bf16[24,1,4,64]{3,0,2,1:T(8,128)(2,1)S(1)} %get-tuple-element.7) | copy-start | bytes 36868
  238.6 5.9 %copy-start.4 = (pred[288,384]{1,0:T(8,128)(4,1)S(1)}, pred[288,384]{1,0:T(8,128)(4,1)}, u32[]{:S(2)}) copy-start(pred[288,384]{1,0:T(8,128)(4,1)} %iota_compare_fusion) | copy-start | bytes 331780
  245.8 15.7 %all-to-all-start.1 = ((f32[1,384,1,4]{3,2,0,1:T(1,128)}), f32[1,384,1,4]{3,2,0,1:T(1,128)S(1)}, u32[]{:S(2)}, u32[]{:S(2)}) async-start(f32[1,384,1,4]{3,2,0,1:T(1,128)} %copy.68), calls=%async_computation.2 | async-start | bytes 393216 | tf_op jit(solution)/shard_map/all_to_all | solution.py:134
  252.9 4.9 %copy-start.13 = (s32[288]{0:T(512)S(1)}, s32[288]{0:T(512)}, u32[]{:S(2)}) copy-start(s32[288]{0:T(512)} %copy-done.12) | copy-start | bytes 3460
  253.0 6.3 %copy-start.15 = (bf16[24,64]{1,0:T(8,128)(2,1)S(1)}, bf16[24,64]{1,0:T(8,128)(2,1)}, u32[]{:S(2)}) copy-start(bf16[24,64]{1,0:T(8,128)(2,1)} %get-tuple-element.10) | copy-start | bytes 9220
  253.0 6.3 %copy-start.16 = (bf16[24,64]{1,0:T(8,128)(2,1)S(1)}, bf16[24,64]{1,0:T(8,128)(2,1)}, u32[]{:S(2)}) copy-start(bf16[24,64]{1,0:T(8,128)(2,1)} %get-tuple-element.11) | copy-start | bytes 9220
  253.0 6.4 %copy-start.7 = (bf16[24,1,4,64]{3,0,2,1:T(8,128)(2,1)S(1)}, bf16[24,1,4,64]{3,0,2,1:T(8,128)(2,1)}, u32[]{:S(2)}) copy-start(bf16[24,1,4,64]{3,0,2,1:T(8,128)(2,1)} %copy-done.6) | copy-start | bytes 36868
  253.0 6.4 %copy-start.9 = (bf16[24,1,4,64]{3,0,2,1:T(8,128)(2,1)S(1)}, bf16[24,1,4,64]{3,0,2,1:T(8,128)(2,1)}, u32[]{:S(2)}) copy-start(bf16[24,1,4,64]{3,0,2,1:T(8,128)(2,1)} %copy-done.8) | copy-start | bytes 36868
  261.5 13.2 %all-to-all-start.2 = ((f32[1,384,1,4]{3,2,0,1:T(1,128)}), f32[1,384,1,4]{3,2,0,1:T(1,128)S(1)}, u32[]{:S(2)}, u32[]{:S(2)}) async-start(f32[1,384,1,4]{3,2,0,1:T(1,128)} %bitcast.101), calls=%async_computation.3 | async-start | bytes 393216 | tf_op jit(solution)/shard_map/all_to_all | solution.py:135
  274.7 0.7 copy-start.3
  275.4 19.0 %all-to-all-start = ((f32[1,384,1,4,128]{4,3,2,0,1:T(4,128)}), f32[1,384,1,4,128]{4,3,2,0,1:T(4,128)}, u32[]{:S(2)}, u32[]{:S(2)}) async-start(f32[1,384,1,4,128]{4,3,2,0,1:T(4,128)} %copy.67), calls=%async_computation.1 | async-start | bytes 1572864 | tf_op jit(solution)/shard_map/all_to_all | solution.py:133
  279.6 110.3 %copy-start.2 = (bf16[48,2560]{1,0:T(8,128)(2,1)S(1)}, bf16[48,2560]{1,0:T(8,128)(2,1)}, u32[]{:S(2)}) copy-start(bf16[48,2560]{1,0:T(8,128)(2,1)} %param.13) | copy-start | bytes 737284
  279.7 110.3 %all-reduce.3.cloned.1.call-start = ((), (), s32[]{:S(2)}) async-start(), calls=%async_computation.5 | async-start | bytes 983040 | tf_op jit(solution)/shard_map/psum | solution.py:163
  280.5 0.6 copy-start.10
  284.5 106.7 %copy-start.17 = (f32[2560]{0:T(1024)S(1)}, f32[2560]{0:T(1024)}, u32[]{:S(2)}) copy-start(f32[2560]{0:T(1024)} %param.23) | copy-start | bytes 30724
  304.2 176.6 %all-reduce.5.cloned.1.call-start = ((), (), s32[]{:S(2)}) async-start(), calls=%async_computation.6 | async-start | bytes 983040 | tf_op jit(solution)/shard_map/psum | solution.py:169
Sparse Core Ops, SparseCore 0:
  14.1 15.5 reduce-scatter.1
  304.3 85.5 all-reduce.2
  397.6 83.0 all-reduce.4
where the time goes:
time: 491 us; the launch traced here: 489 us
  local copies, waits for them, and re-layouts  194 us (40%)
  waiting for transfers between devices  181 us (37%)
  blocking collectives  36.5 us (7%)
  matrix products  27.1 us (6%)
  other arithmetic  22.4 us (5%)
  between operations  14.1 us (3%)
  starting transfers between devices  13.6 us (3%)
    scatter x1, local copies, waits for them, and re-layouts, per_device(): block_all = jnp.zeros((holder_count * slot_count,), jnp.int32).at[target]...  90.5 us
    scatter x1, local copies, waits for them, and re-layouts, per_device(): owner_all = jnp.full((holder_count * slot_count,), -1, jnp.int32).at[targ...  90.2 us
    psum x1, waiting for transfers between devices, per_device(): mixed = lax.psum(partial_out, 'wide')  85.7 us
    psum x1, waiting for transfers between devices, per_device(): lax.psum(down, ('wide', 'narrow'))  83.2 us
    all_gather x1, blocking collectives, per_device(): all_queries = lax.all_gather(query, ('pool', 'narrow'), axis=0, tiled=True)  32 us
  transfers between devices with their start and end apart: 6, of which 4 were waited for; matrix products, arithmetic and copies ran while one was open for 42% of the time, Pallas kernels for 0%

commit v1 on v0

--- a/solution.py
+++ b/solution.py
@@ -166,7 +166,7 @@
     normed_post = rms_scale(resid, gain_post).astype(jnp.bfloat16)
     hidden = feed_forward(normed_post, w_gate_up)
     down = jnp.dot(hidden, w_down, preferred_element_type=jnp.float32)
-    layer_out = (resid + lax.psum(down, ("wide", "narrow"))).astype(jnp.bfloat16)
+    layer_out = (resid + lax.psum(lax.psum(down, "narrow"), "wide")).astype(jnp.bfloat16)
     return (attn_mixed, layer_out)
 
 

time: 491 us -> 529 us (1.077)
  waiting for transfers between devices: 181 us -> 220 us
    psum x1 -> x2, waiting for transfers between devices: 83.2 us -> 121 us  [the longest x1 89.1 us: per_device(): lax.psum(lax.psum(down, 'narrow'), 'wide')]
  transfers between devices with their start and end apart: 6 -> 7, of which waited for: 4 -> 5; matrix products, arithmetic and copies ran while one was open for 42% -> 39% of each run, Pallas kernels for 0% -> 0%
where the time goes in v1:
time: 529 us; the launch traced here: 528 us
  waiting for transfers between devices  220 us (42%)
  local copies, waits for them, and re-layouts  194 us (37%)
  blocking collectives  36.5 us (7%)
  matrix products  27.1 us (5%)
  other arithmetic  22.4 us (4%)
  between operations  14.1 us (3%)
  starting transfers between devices  13.6 us (3%)
    scatter x1, local copies, waits for them, and re-layouts, per_device(): block_all = jnp.zeros((holder_count * slot_count,), jnp.int32).at[target]...  90.5 us
    scatter x1, local copies, waits for them, and re-layouts, per_device(): owner_all = jnp.full((holder_count * slot_count,), -1, jnp.int32).at[targ...  90.2 us
    psum x1, waiting for transfers between devices, per_device(): lax.psum(lax.psum(down, 'narrow'), 'wide')  89.1 us
    psum x1, waiting for transfers between devices, per_device(): mixed = lax.psum(partial_out, 'wide')  85.7 us
    psum x1, waiting for transfers between devices, per_device(): lax.psum(down, 'narrow')  32.3 us
    all_gather x1, blocking collectives, per_device(): all_queries = lax.all_gather(query, ('pool', 'narrow'), axis=0, tiled=True)  32 us
  transfers between devices with their start and end apart: 7, of which 5 were waited for; matrix products, arithmetic and copies ran while one was open for 39% of the time, Pallas kernels for 0%

profile of v1, /device:TPU:0, one launch (start us, length us, event | category | flops | bytes accessed | tf_op | source)
XLA Modules:
  0.0 527.7 jit_solution(267179423901199933)
XLA Ops:
  7.2 1.2 multiply_reduce_fusion.1
  8.5 1.8 convert_element_type.67
  10.3 0.8 dynamic-slice
  11.0 2.9 fusion.9
  14.0 0.7 fusion.32
  15.1 90.5 %scatter_custom_fusion.1 = s32[2304]{0:T(1024)S(1)} fusion(s32[24576]{0:T(1024)S(1)} %bitcast.105, s32[24576]{0:T(1024)} %fusion.32, s32[]{:T(128)} %constant.29.clone.1), kind=kCustom, calls=%fused_computation.110 | custom fusion | bytes 9728 | tf_op jit(solution)/shard_map/scatter | solution.py:88
  105.6 90.2 %scatter_custom_fusion = s32[2304]{0:T(1024)S(1)} fusion(s32[24576]{0:T(1024)S(1)} %bitcast.106, s32[24576]{0:T(1024)S(1)} %add_select_fusion, s32[]{:T(128)} %constant.28.clone.1), kind=kCustom, calls=%fused_computation.112 | custom fusion | bytes 9220 | tf_op jit(solution)/shard_map/scatter | solution.py:83
  196.0 2.4 gather_fusion
  198.7 0.8 iota_compare_fusion
  199.5 0.8 multiply_reduce_fusion.4
  200.3 0.9 multiply_reduce_fusion.3
  201.2 0.8 multiply_multiply_fusion.1
  202.0 0.7 fusion.76
  202.8 0.9 multiply_multiply_fusion
  203.9 32.0 %all_gather.6 = bf16[384,1,4,128]{3,0,2,1:T(8,128)(2,1)S(1)} all-gather(bf16[24,1,4,128]{3,0,2,1:T(8,128)(2,1)S(1)} %pad_maximum_fusion), channel_id=1, replica_groups=mesh['pool'=8,'wide'=8,'narrow'=2] {'pool','narrow'}, dimensions={0}, use_global_device_ids=true | all-gather | bytes 417792 | tf_op jit(solution)/shard_map/all_gather | solution.py:71
  236.2 2.4 gather_fusion.1
  238.6 5.8 %select_reduce_fusion.1 = (f32[288,4]{1,0:T(8,128)S(1)}, f32[288,4,64]{2,1,0:T(4,128)}) fusion(pred[288,64]{1,0:T(8,128)(4,1)S(1)} %fusion.36, bf16[288,4,128]{2,1,0:T(4,128)(2,1)} %gather_fusion.1, bf16[288,1,64,128]{3,2,1,0:T(8,128)(2,1)} %param.18), kind=kOutput, calls=%fused_computation.23 | convolution fusion | flops 19094400 | bytes 5331456 | tf_op jit(solution)/shard_map/skgd,sktd->skgt/dot_general | solution.py:103
  245.0 0.8 copy.68
  245.8 3.5 all-to-all-start.1
  249.3 1.7 gather_fusion.2
  251.1 1.9 fusion.16
  253.0 4.8 fusion
  257.9 1.4 fusion.29
  259.5 0.8 fusion.58
  260.2 1.3 fusion.70
  261.5 5.6 %all-to-all-start.2 = ((f32[1,384,1,4]{3,2,0,1:T(1,128)}), f32[1,384,1,4]{3,2,0,1:T(1,128)S(1)}, u32[]{:S(2)}, u32[]{:S(2)}) async-start(f32[1,384,1,4]{3,2,0,1:T(1,128)} %bitcast.101), calls=%async_computation.3 | async-start | bytes 393216 | tf_op jit(solution)/shard_map/all_to_all | solution.py:135
  267.2 2.0 convolution_bitcast_fusion
  269.1 1.4 copy.67
  271.2 3.5 all-to-all-done.2
  274.7 0.7 copy-done.3
  275.4 4.3 all-to-all-start
  279.7 0.8 multiply_maximum_fusion
  281.1 0.7 subtract_exponential_fusion
  281.8 1.7 copy.69
  283.5 1.0 multiply_reduce_fusion.2
  284.5 0.7 convert_convert_fusion
  285.4 8.9 %all-to-all-done = f32[1,384,1,4,128]{4,3,2,0,1:T(4,128)} async-done(((f32[1,384,1,4,128]{4,3,2,0,1:T(4,128)}), f32[1,384,1,4,128]{4,3,2,0,1:T(4,128)}, u32[]{:S(2)}, u32[]{:S(2)}) %all-to-all-start) | async-done | bytes 786464 | tf_op jit(solution)/shard_map/all_to_all | solution.py:133
  294.3 1.4 fusion.12
  295.7 0.8 copy_bitcast_fusion
  296.5 4.5 all_gather.7
  301.0 3.1 fusion.81
  304.2 85.7 %all-reduce.4.cloned.1.call-done = f32[48,2560]{1,0:T(8,128)} async-done(((f32[48,2560]{1,0:T(8,128)}), f32[48,2560]{1,0:T(8,128)}) %all-reduce.4.cloned.1.call-update) | async-done | bytes 491536 | tf_op jit(solution)/shard_map/psum | solution.py:163
  389.9 1.2 multiply_reduce_fusion
  391.1 4.9 fusion.23
  396.1 1.4 fusion.50
  397.6 32.3 %all-reduce.6.cloned.1.call-done = f32[48,2560]{1,0:T(8,128)} async-done(((f32[48,2560]{1,0:T(8,128)}), f32[48,2560]{1,0:T(8,128)}) %all-reduce.6.cloned.1.call-update) | async-done | bytes 491536 | tf_op jit(solution)/shard_map/psum | solution.py:169
  429.9 89.1 %all-reduce.8.cloned.1.call-done = f32[48,2560]{1,0:T(8,128)} async-done(((f32[48,2560]{1,0:T(8,128)}), f32[48,2560]{1,0:T(8,128)}) %all-reduce.8.cloned.1.call-update) | async-done | bytes 491536 | tf_op jit(solution)/shard_map/psum | solution.py:169
  519.0 2.2 add_convert_fusion
  (73 shorter events, 3.8 us)
Async XLA Ops:
  7.2 388.9 %copy-start = (bf16[608,2560]{1,0:T(8,128)(2,1)S(1)}, bf16[608,2560]{1,0:T(8,128)(2,1)}, u32[]{:S(2)}) copy-start(bf16[608,2560]{1,0:T(8,128)(2,1)} %param.25) | copy-start | bytes 9338884
  7.2 7.4 %copy-start.11 = (s32[384,64]{0,1:T(8,128)S(1)}, s32[384,64]{0,1:T(8,128)}, u32[]{:S(2)}) copy-start(s32[384,64]{0,1:T(8,128)} %param.21) | copy-start | bytes 294916
  7.2 188.8 %copy-start.1 = (s32[384]{0:T(512)S(1)}, s32[384]{0:T(512)}, u32[]{:S(2)}) copy-start(s32[384]{0:T(512)} %param.20) | copy-start | bytes 4612
  7.2 192.3 %reduce-scatter.2.cloned.1.call-start = ((), (), s32[]{:S(2)}) async-start(), calls=%async_computation.4 | async-start | bytes 221184 | tf_op jit(solution)/shard_map/reduce_scatter | solution.py:60
  10.3 192.5 %copy-start.18 = (f32[128]{0:T(128)S(1)}, f32[128]{0:T(128)}, u32[]{:S(2)}) copy-start(f32[128]{0:T(128)} %param.16) | copy-start | bytes 1540
  195.9 40.0 %copy-start.12 = (s32[288]{0:T(512)}, s32[288]{0:T(512)S(1)}, u32[]{:S(2)}) copy-start(s32[288]{0:T(512)S(1)} %get-tuple-element.3) | copy-start | bytes 3460
  195.9 48.5 %copy-start.14 = (s32[1024]{0:T(1024)}, s32[1024]{0:T(1024)S(1)}, u32[]{:S(2)}) copy-start(s32[1024]{0:T(1024)S(1)} %pad_clamp_fusion) | copy-start | bytes 12292
  198.6 45.8 %copy-start.5 = (pred[288,64]{1,0:T(8,128)(4,1)}, pred[288,64]{1,0:T(8,128)(4,1)S(1)}, u32[]{:S(2)}) copy-start(pred[288,64]{1,0:T(8,128)(4,1)S(1)} %fusion.36) | copy-start | bytes 55300
  203.8 32.1 %copy-start.6 = (bf16[24,1,4,64]{3,0,2,1:T(8,128)(2,1)}, bf16[24,1,4,64]{3,0,2,1:T(8,128)(2,1)S(1)}, u32[]{:S(2)}) copy-start(bf16[24,1,4,64]{3,0,2,1:T(8,128)(2,1)S(1)} %get-tuple-element.6) | copy-start | bytes 36868
  203.8 32.1 %copy-start.8 = (bf16[24,1,4,64]{3,0,2,1:T(8,128)(2,1)}, bf16[24,1,4,64]{3,0,2,1:T(8,128)(2,1)S(1)}, u32[]{:S(2)}) copy-start(bf16[24,1,4,64]{3,0,2,1:T(8,128)(2,1)S(1)} %get-tuple-element.7) | copy-start | bytes 36868
  238.6 5.9 %copy-start.4 = (pred[288,384]{1,0:T(8,128)(4,1)S(1)}, pred[288,384]{1,0:T(8,128)(4,1)}, u32[]{:S(2)}) copy-start(pred[288,384]{1,0:T(8,128)(4,1)} %iota_compare_fusion) | copy-start | bytes 331780
  245.8 15.7 %all-to-all-start.1 = ((f32[1,384,1,4]{3,2,0,1:T(1,128)}), f32[1,384,1,4]{3,2,0,1:T(1,128)S(1)}, u32[]{:S(2)}, u32[]{:S(2)}) async-start(f32[1,384,1,4]{3,2,0,1:T(1,128)} %copy.68), calls=%async_computation.2 | async-start | bytes 393216 | tf_op jit(solution)/shard_map/all_to_all | solution.py:134
  252.9 4.9 copy-start.13
  253.0 6.3 %copy-start.15 = (bf16[24,64]{1,0:T(8,128)(2,1)S(1)}, bf16[24,64]{1,0:T(8,128)(2,1)}, u32[]{:S(2)}) copy-start(bf16[24,64]{1,0:T(8,128)(2,1)} %get-tuple-element.10) | copy-start | bytes 9220
  253.0 6.3 %copy-start.16 = (bf16[24,64]{1,0:T(8,128)(2,1)S(1)}, bf16[24,64]{1,0:T(8,128)(2,1)}, u32[]{:S(2)}) copy-start(bf16[24,64]{1,0:T(8,128)(2,1)} %get-tuple-element.11) | copy-start | bytes 9220
  253.0 6.4 %copy-start.7 = (bf16[24,1,4,64]{3,0,2,1:T(8,128)(2,1)S(1)}, bf16[24,1,4,64]{3,0,2,1:T(8,128)(2,1)}, u32[]{:S(2)}) copy-start(bf16[24,1,4,64]{3,0,2,1:T(8,128)(2,1)} %copy-done.6) | copy-start | bytes 36868
  253.0 6.4 %copy-start.9 = (bf16[24,1,4,64]{3,0,2,1:T(8,128)(2,1)S(1)}, bf16[24,1,4,64]{3,0,2,1:T(8,128)(2,1)}, u32[]{:S(2)}) copy-start(bf16[24,1,4,64]{3,0,2,1:T(8,128)(2,1)} %copy-done.8) | copy-start | bytes 36868
  261.5 13.2 %all-to-all-start.2 = ((f32[1,384,1,4]{3,2,0,1:T(1,128)}), f32[1,384,1,4]{3,2,0,1:T(1,128)S(1)}, u32[]{:S(2)}, u32[]{:S(2)}) async-start(f32[1,384,1,4]{3,2,0,1:T(1,128)} %bitcast.101), calls=%async_computation.3 | async-start | bytes 393216 | tf_op jit(solution)/shard_map/all_to_all | solution.py:135
  274.7 0.7 copy-start.3
  275.4 19.0 %all-to-all-start = ((f32[1,384,1,4,128]{4,3,2,0,1:T(4,128)}), f32[1,384,1,4,128]{4,3,2,0,1:T(4,128)}, u32[]{:S(2)}, u32[]{:S(2)}) async-start(f32[1,384,1,4,128]{4,3,2,0,1:T(4,128)} %copy.67), calls=%async_computation.1 | async-start | bytes 1572864 | tf_op jit(solution)/shard_map/all_to_all | solution.py:133
  279.6 110.3 %copy-start.2 = (bf16[48,2560]{1,0:T(8,128)(2,1)S(1)}, bf16[48,2560]{1,0:T(8,128)(2,1)}, u32[]{:S(2)}) copy-start(bf16[48,2560]{1,0:T(8,128)(2,1)} %param.13) | copy-start | bytes 737284
  279.7 110.3 %all-reduce.4.cloned.1.call-start = ((), (), s32[]{:S(2)}) async-start(), calls=%async_computation.5 | async-start | bytes 983040 | tf_op jit(solution)/shard_map/psum | solution.py:163
  280.5 0.6 copy-start.10
  284.5 106.7 %copy-start.17 = (f32[2560]{0:T(1024)S(1)}, f32[2560]{0:T(1024)}, u32[]{:S(2)}) copy-start(f32[2560]{0:T(1024)} %param.23) | copy-start | bytes 30724
  304.2 125.7 %all-reduce.6.cloned.1.call-start = ((), (), s32[]{:S(2)}) async-start(), calls=%async_computation.6 | async-start | bytes 983040 | tf_op jit(solution)/shard_map/psum | solution.py:169
  397.5 121.5 %all-reduce.8.cloned.1.call-start = ((), (), s32[]{:S(2)}) async-start(), calls=%async_computation.7 | async-start | bytes 983040 | tf_op jit(solution)/shard_map/psum | solution.py:169
Sparse Core Ops, SparseCore 0:
  14.1 15.5 reduce-scatter.1
  304.3 85.5 all-reduce.3
  397.6 32.1 all-reduce.5
  432.4 86.5 all-reduce.7
